TPU v7x, 512 devices: a whole 4x8x8 slice. The times are simulated.
512 devices in a mesh: body: 32 (over y, x), surf: 16 (over z, core).
Axes of the slice: x: 4, y: 8, z: 8, core: 2. Of those that a mesh axis runs over, the one named last changes fastest.
Arguments:
- body_panels: float32 [12, 96, 2048], P(None, 'body', 'surf'), may hold values from -6 to 192, as said below
- body_normals: float32 [3, 96, 2048], P(None, 'body', 'surf'), may hold values from -3 to 3
- fs_panels: float32 [4, 65536], P(None, ('body', 'surf')), may hold values from -6 to 192, as said below
- fs_state: float32 [2, 65536], P(None, ('body', 'surf')), may hold values from -6 to 6
- pairs: int32 [72, 2], replicated, may hold values from 0 to 95, as said below
Outputs:
- body_potential: float32 [96, 8, 2048], P('body', None, 'surf')
- body_force: float32 [96, 8, 3], P('body')
- fs_next: float32 [2, 65536], P(None, ('body', 'surf'))
Inputs may be any that keep to these rules, and one draw needn't show every extreme that they name: Rows are distinct pairs (i, j) with i < j <= i + 3, ordered by i and then by j. `body_panels`: body b's centroids lie within x in 2 b - 1 to 2 b + 1, y in -1 to 1, z in -2 to -1; areas are positive; source strengths are within -6 to 6. `fs_panels`: Free-surface panels of group g have x in 2 * 3 g - 1 to 2 * 3 (g + 1) - 1, y in -3 to 3, positive areas, source strengths within -6 to 6.
All inputs are finite; a program needn't handle non-finite values.
Results may differ from a plain program's by a relative error of at most 0.0003.
Values sent between devices are 32-bit elements; how exact they have to be, the bound alone decides.
A program may use at most 64 MiB of HBM per device.

v0:
```python
import functools

import jax
import jax.numpy as jnp
from jax import lax
from jax.experimental import pallas as pl
from jax.experimental.pallas import tpu as pltpu
from jax.sharding import PartitionSpec as P

MESH = pl.DeviceIdType.MESH
F32 = jnp.float32
BF16 = jnp.bfloat16
SOFTEN = 0.01
GRAVITY = 9.81
STEP = 0.2
DEPTH = 1.5

CROSS = [
    [(+1, t) for t in range(b + 1)] + [(-1, t) for t in range(b, 3)] for b in range(3)
]
PAIRS = [(0, 1), (0, 2), (1, 2)]
PAIRS += [(b, 3 + t) for b in range(3) for t in range(b + 1)]
PAIRS += [(t - 3, b) for b in range(3) for t in range(b, 3)]


def rounded(x):
    return x.astype(BF16).astype(F32)


def split3(x):
    a = rounded(x)
    r = x - a
    b = rounded(r)
    return a, b, rounded(r - b)


def split2(x):
    a = rounded(x)
    return jnp.concatenate([a, x - a], axis=0).astype(BF16)


def kernel(
    nz,
    bp, bn, fsp, fst, prs,
    pot, force, fsn,
    pay, nbr, tgt, tgf, ft, acc, accf, reto, reti, msk, frc,
    s_dir, r_dir, s_rel, r_rel, s_nb, r_nb, s_ret, r_ret, s_f, r_f,
):
    groups = lax.axis_size("body")
    tiles = 2 * nz
    g = lax.axis_index("body")
    s = lax.axis_index("surf")
    z, core = s // 2, lax.rem(s, 2)
    partner = 2 * z + 1 - core
    following = lax.rem(g + 1, groups)
    preceding = lax.rem(g + groups - 1, groups)

    barrier = pltpu.get_barrier_semaphore()
    for d in range(1, tiles):
        pl.semaphore_signal(
            barrier, inc=1, device_id=(g, lax.rem(s + d, tiles)), device_id_type=MESH
        )
    for other in (following, preceding):
        pl.semaphore_signal(barrier, inc=1, device_id=(other, s), device_id_type=MESH)

    base = 6.0 * g.astype(F32)
    area = bp[3]
    for k in range(8):
        w = bp[4 + k] * area
        for b in range(3):
            pay[0, 0, 8 * b + k : 8 * b + k + 1, :] = w[b : b + 1, :]
    for b in range(3):
        x = bp[0, b : b + 1, :] - (base + 2.0 * b)
        y = bp[1, b : b + 1, :]
        zz = bp[2, b : b + 1, :] + DEPTH
        for i, v in enumerate((x, y, zz, x * x + y * y + zz * zz)):
            pay[0, 0, 24 + 4 * b + i : 25 + 4 * b + i, :] = v
    fx = fsp[0:1, :] - (base + 2.0)
    fy = fsp[1:2, :]
    for i, v in enumerate((fx, fy, fsp[2:3, :] * fsp[3:4, :], fx * fx + fy * fy)):
        pay[0, 0, 36 + i : 37 + i, :] = v

    pl.semaphore_wait(barrier, tiles + 1)

    def direct(o):
        return pltpu.make_async_remote_copy(
            src_ref=pay.at[0, 0], dst_ref=pay.at[o, 0],
            send_sem=s_dir.at[o], recv_sem=r_dir.at[o],
            device_id=(g, 2 * lax.rem(z + o, nz) + core), device_id_type=MESH,
        )

    def relay(o):
        return pltpu.make_async_remote_copy(
            src_ref=pay.at[o, 0], dst_ref=pay.at[o, 1],
            send_sem=s_rel.at[o], recv_sem=r_rel.at[o],
            device_id=(g, partner), device_id_type=MESH,
        )

    def points(i):
        return pltpu.make_async_remote_copy(
            src_ref=pay.at[0, 0, pl.ds(24, 16)], dst_ref=nbr.at[i],
            send_sem=s_nb.at[i], recv_sem=r_nb.at[i],
            device_id=((following, preceding)[i], s), device_id_type=MESH,
        )

    def give_back(i):
        return pltpu.make_async_remote_copy(
            src_ref=reto.at[i], dst_ref=reti.at[i],
            send_sem=s_ret.at[i], recv_sem=r_ret.at[i],
            device_id=((following, preceding)[i], s), device_id_type=MESH,
        )

    def forces(d, slot):
        return pltpu.make_async_remote_copy(
            src_ref=frc.at[slot], dst_ref=frc.at[slot],
            send_sem=s_f.at[d], recv_sem=r_f.at[slot],
            device_id=(g, lax.rem(s + d, tiles)), device_id_type=MESH,
        )

    def order(k):
        half = (k + 1) // 2
        return jnp.where(lax.rem(k, 2) == 1, half, lax.rem(nz - half, nz))

    points(0).start()
    points(1).start()
    relay(0).start()
    for h in range(1, nz // 2 + 1):
        direct(h).start()
        if h != nz - h:
            direct(nz - h).start()

    row_i = lax.broadcasted_iota(jnp.int32, (16, prs.shape[1]), 0)
    first = jnp.full(row_i.shape, -9, jnp.int32)
    second = first
    for r, (i, j) in enumerate(PAIRS):
        first = jnp.where(row_i == r, i, first)
        second = jnp.where(row_i == r, j, second)
    found = (prs[0:1, :] == first + 3 * g) & (prs[1:2, :] == second + 3 * g)
    hit = jnp.sum(jnp.where(found, 1.0, 0.0), axis=1, keepdims=True)
    msk[...] = jnp.broadcast_to(hit, (16, 128))

    def allowed(i, j):
        r = PAIRS.index((i, j))
        return jnp.broadcast_to(msk[r : r + 1, :], (8, 128))

    row8 = lax.broadcasted_iota(jnp.int32, (8, 128), 0)

    def put_target(ref, at, x, y, zz, top, use_z=True):
        m = x * x + y * y + zz * zz + SOFTEN
        o = 0 if top else 4
        t = jnp.where(row8 == o, -2.0 * x, 0.0)
        t = jnp.where(row8 == o + 1, -2.0 * y, t)
        if use_z:
            t = jnp.where(row8 == o + 2, -2.0 * zz, t)
        t = jnp.where(row8 == o + 3, 1.0, t)
        t = jnp.where(row8 == 4 - o, m, t)
        t1, t2, t3 = split3(t)
        ref[:, 128 * at : 128 * at + 128] = jnp.concatenate(
            [t1, t2, t1, t2, t3, t1], axis=0
        ).astype(BF16)

    def spread(ref, r):
        return jnp.broadcast_to(ref[r : r + 1, :], (8, 128))

    def target(b, at, ref, r, shift):
        put_target(
            tgt.at[b], at, spread(ref, r) + 2.0 * shift, spread(ref, r + 1),
            spread(ref, r + 2), b != 1,
        )

    mine = pay.at[0, 0]
    for b in range(3):
        for t in range(3):
            target(b, 4 + t, mine, 24 + 4 * t, t - b)
        put_target(
            tgt.at[b], 7, spread(mine, 36) + 2.0 * (1 - b), spread(mine, 37),
            jnp.full((8, 128), DEPTH, F32), b != 1,
        )
    for t in range(3):
        put_target(
            tgf, t, spread(mine, 24 + 4 * t) + 2.0 * (t - 1), spread(mine, 25 + 4 * t),
            spread(mine, 26 + 4 * t) - DEPTH, False, use_z=False,
        )

    acc[...] = jnp.zeros_like(acc)
    accf[...] = jnp.zeros_like(accf)

    points(0).wait_recv()
    points(1).wait_recv()
    for b in range(3):
        for at, (side, t) in enumerate(CROSS[b]):
            target(b, at, nbr.at[0 if side < 0 else 1], 4 * t, 3 * side + t - b)

    row = lax.broadcasted_iota(jnp.int32, (8, 256), 0)

    def both(o, r):
        return jnp.concatenate([pay[o, 0, r : r + 8, :], pay[o, 1, r : r + 8, :]], axis=1)

    def sources(o):
        p, q = both(o, 24), both(o, 32)
        low = row < 4
        one4 = jnp.where(row == 4, 1.0, 0.0)
        one0 = jnp.where(row == 0, 1.0, 0.0)
        for i, c in enumerate(
            (jnp.where(low, p, one4), jnp.where(low, one0, p),
             jnp.where(low, q, one4), jnp.where(low, one0, q))
        ):
            c1, c2, c3 = split3(c)
            f = jnp.concatenate([c1, c1, c2, c2, c1, c3], axis=0)
            ft[o, i] = f.T.astype(BF16)

    def sweep(features, targets, lhs, cubed=False):
        total = None
        for c in range(2):
            rows = features[128 * c : 128 * c + 128, :]
            left = lhs[:, 128 * c : 128 * c + 128]
            d2 = jnp.dot(rows, targets, preferred_element_type=F32)
            k = lax.rsqrt(d2)
            if cubed:
                k = k * k * k
            hi = k.astype(BF16)
            lo = (k - hi.astype(F32)).astype(BF16)
            part = jnp.dot(left, hi, preferred_element_type=F32)
            part += jnp.dot(left, lo, preferred_element_type=F32)
            total = part if total is None else total + part
        return total

    def cross_step(k, carry):
        o = order(k)

        @pl.when(k < nz - 1)
        def _():
            ahead = order(k + 1)
            direct(ahead).wait_recv()
            relay(ahead).start()

        relay(o).wait_recv()
        sources(o)
        for b in range(3):
            lhs = split2(both(o, 8 * b))
            for n in (0, 256):
                acc[b, :, n : n + 256] += sweep(ft.at[o, b], tgt[b, :, n : n + 256], lhs)
        return carry

    lax.fori_loop(0, nz, cross_step, 0)

    def result(b, at):
        lanes = pl.ds(128 * at, 128)
        return acc[b, 0:8, lanes] + acc[b, 8:16, lanes]

    for i, side in enumerate((+1, -1)):
        for t in range(3):
            total = jnp.zeros((8, 128), F32)
            for b in range(3):
                if (side, t) in CROSS[b]:
                    pair = (b, 3 + t) if side > 0 else (t - 3, b)
                    total += result(b, CROSS[b].index((side, t))) * allowed(*pair)
            reto[i, t] = total
    give_back(0).start()
    give_back(1).start()

    def own_step(o, carry):
        for b in range(3):
            lhs = split2(both(o, 8 * b))
            for n, width in ((512, 256), (768, 128)):
                acc[b, :, n : n + width] += sweep(ft.at[o, b], tgt[b, :, n : n + width], lhs)
        lhs = split2(both(o, 32))
        for n, width in ((0, 256), (256, 128)):
            accf[:, n : n + width] += sweep(ft.at[o, 3], tgf[:, n : n + width], lhs)
        return carry

    lax.fori_loop(0, nz, own_step, 0)

    give_back(0).wait_recv()
    give_back(1).wait_recv()
    lane = lax.broadcasted_iota(jnp.int32, (8, 128), 1)
    packed = jnp.zeros((8, 128), F32)
    for t in range(3):
        total = reti[0, t] + reti[1, t]
        for b in range(3):
            r = result(b, 4 + t)
            total += r if b == t else r * allowed(min(b, t), max(b, t))
        surface = accf[6:7, 128 * t : 128 * t + 128] + accf[14:15, 128 * t : 128 * t + 128]
        total += jnp.where(row8 == 0, surface, 0.0)
        pot[t] = total
        for k in range(3):
            an = bn[k, t : t + 1, :] * bp[3, t : t + 1, :]
            column = jnp.sum(total * an, axis=1, keepdims=True)
            packed = jnp.where(lane == 16 * row8 + 3 * t + k, column, packed)
    frc[s] = jnp.sum(packed, axis=0, keepdims=True)
    for d in range(1, tiles):
        forces(d, s).start()

    def velocity_step(o, carry):
        for b in range(3):
            tile = both(o, 24 if b < 2 else 32)
            w0 = jnp.broadcast_to(both(o, 8 * b)[0:1, :], (8, 256))
            r = 4 if b == 1 else 0
            lhs = split2(w0 * jnp.where(row == r + 3, 1.0, tile))
            acc[b, :, 896:1024] += sweep(ft.at[o, b], tgt[b, :, 896:1024], lhs, cubed=True)
        return carry

    lax.fori_loop(0, nz, velocity_step, 0)

    v = [jnp.zeros((1, 128), F32)] * 3
    for b in range(3):
        moments = result(b, 7)
        r = 4 if b == 1 else 0
        point = (pay[0, 0, 36:37, :] + 2.0 * (1 - b), pay[0, 0, 37:38, :], DEPTH)
        for i in range(3):
            v[i] = v[i] + (moments[r + i : r + i + 1] - point[i] * moments[r + 3 : r + 4])
    speed_sq = v[0] * v[0] + v[1] * v[1] + v[2] * v[2]
    phi, eta = fst[0:1, :], fst[1:2, :]
    fsn[0:1, :] = phi + STEP * (-GRAVITY * eta - 0.5 * speed_sq)
    fsn[1:2, :] = eta + STEP * v[2]

    for d in range(1, tiles):
        forces(0, lax.rem(s + d, tiles)).wait_recv()
    whole = frc[0]
    for i in range(1, tiles):
        whole = whole + frc[i]
    whole = jnp.broadcast_to(whole, (8, 128))
    for t in range(3):
        for k in range(3):
            force[t, :, k : k + 1] = jnp.sum(
                jnp.where(lane == 16 * row8 + 3 * t + k, whole, 0.0), axis=1, keepdims=True
            )

    for i in range(2):
        points(i).wait_send()
        give_back(i).wait_send()
    for o in range(nz):
        relay(o).wait_send()
        if o:
            direct(o).wait_send()
    for d in range(1, tiles):
        forces(d, s).wait_send()


def on_device(bp, bn, fsp, fst, pairs):
    nz = lax.axis_size("surf") // 2
    tiles = 2 * nz
    dma = pltpu.SemaphoreType.DMA
    vmem = pl.BlockSpec(memory_space=pltpu.VMEM)
    return pl.pallas_call(
        functools.partial(kernel, nz),
        out_shape=(
            jax.ShapeDtypeStruct((3, 8, 128), F32),
            jax.ShapeDtypeStruct((3, 8, 3), F32),
            jax.ShapeDtypeStruct((2, 128), F32),
        ),
        in_specs=[vmem] * 5,
        out_specs=(vmem,) * 3,
        scratch_shapes=[
            pltpu.VMEM((nz, 2, 40, 128), F32),
            pltpu.VMEM((2, 16, 128), F32),
            pltpu.VMEM((3, 48, 1024), BF16),
            pltpu.VMEM((48, 384), BF16),
            pltpu.VMEM((nz, 4, 256, 48), BF16),
            pltpu.VMEM((3, 16, 1024), F32),
            pltpu.VMEM((16, 384), F32),
            pltpu.VMEM((2, 3, 8, 128), F32),
            pltpu.VMEM((2, 3, 8, 128), F32),
            pltpu.VMEM((16, 128), F32),
            pltpu.VMEM((tiles, 1, 128), F32),
            dma((nz,)), dma((nz,)), dma((nz,)), dma((nz,)),
            dma((2,)), dma((2,)), dma((2,)), dma((2,)),
            dma((tiles,)), dma((tiles,)),
        ],
        compiler_params=pltpu.CompilerParams(collective_id=0, has_side_effects=True),
        name="section",
    )(bp, bn, fsp, fst, pairs.T)


def solution(mesh):
    placed = (
        P(None, "body", "surf"),
        P(None, "body", "surf"),
        P(None, ("body", "surf")),
        P(None, ("body", "surf")),
        P(),
    )
    return jax.shard_map(
        on_device,
        mesh=mesh,
        in_specs=placed,
        out_specs=(P("body", None, "surf"), P("body", None, None), P(None, ("body", "surf"))),
        check_vma=False,
    )
```

profile of v0, /device:TPU:1, one launch (start us, length us, event | category | flops | bytes accessed | tf_op | source)
XLA Modules:
  0.0 52.7 jit_solution(11515468116976457519)
XLA Ops:
  0.6 49.4 %section.1 = (f32[3,8,128]{2,1,0:T(8,128)}, f32[3,8,3]{2,1,0:T(8,128)}, f32[2,128]{1,0:T(2,128)}) custom-call(f32[12,3,128]{2,1,0:T(4,128)} %bp.1, f32[3,3,128]{2,1,0:T(4,128)} %bn.1, f32[4,128]{1,0:T(4,128)} %fsp.1, f32[2,128]{1,0:T(2,128)} %fst.1, s32[2,72]{1,0:T(2,128)} %bitcast.1), custom_call_target="tpu_custom_call" | custom-call | tf_op jit(solution)/shard_map/section/pallas_call | solution.py:345
  50.1 0.0 copy-start
  50.1 1.4 %copy.8 = f32[3,8,3]{1,2,0:T(4,128)} copy(f32[3,8,3]{2,1,0:T(8,128)} %get-tuple-element.4) | data formatting | bytes 576 | tf_op jit(solution)/shard_map/section/pallas_call | solution.py:345
  51.5 0.0 copy-done
  51.5 0.0 copy-start.1
  51.5 0.6 %copy.11 = f32[3,8,128]{2,1,0:T(8,128)} copy(f32[3,8,128]{2,1,0:T(8,128)S(1)} %copy-done) | data formatting | bytes 24576
  52.1 0.0 copy-done.1
  52.1 0.6 %copy.12 = f32[2,128]{1,0:T(2,128)} copy(f32[2,128]{1,0:T(2,128)S(1)} %copy-done.1) | data formatting | bytes 2048
Async XLA Ops:
  50.1 1.4 %copy-start = (f32[3,8,128]{2,1,0:T(8,128)S(1)}, f32[3,8,128]{2,1,0:T(8,128)}, u32[]{:S(2)}) copy-start(f32[3,8,128]{2,1,0:T(8,128)} %get-tuple-element.9) | copy-start | bytes 36868
  51.5 0.6 %copy-start.1 = (f32[2,128]{1,0:T(2,128)S(1)}, f32[2,128]{1,0:T(2,128)}, u32[]{:S(2)}) copy-start(f32[2,128]{1,0:T(2,128)} %get-tuple-element.11) | copy-start | bytes 3076
where the time goes:
time: 52.9 us; the launch traced here: 52.7 us
  Pallas kernels  49.4 us (93%)
  local copies, waits for them, and re-layouts  2.59 us (5%)
  between operations  0.65 us (1%)
    pallas_call x1, Pallas kernels, on_device(): pl.pallas_call(functools.partial(kernel, nz), out_shape=(jax.ShapeDtypeSt...  49.4 us
    pallas_call x1, local copies, waits for them, and re-layouts, on_device(): pl.pallas_call(functools.partial(kernel, nz), out_shape=(jax.ShapeDtypeSt...  1.39 us
    unnamed x6, local copies, waits for them, and re-layouts  1.2 us

commit v1 on v0

--- a/solution.py
+++ b/solution.py
@@ -43,7 +43,7 @@
     nz,
     bp, bn, fsp, fst, prs,
     pot, force, fsn,
-    pay, nbr, tgt, tgf, ft, acc, accf, reto, reti, msk, frc,
+    pay, nbr, tgt, tgp, tgf, tgv, ft, acc, accp, accf, accv, accw, reto, reti, msk, frc,
     s_dir, r_dir, s_rel, r_rel, s_nb, r_nb, s_ret, r_ret, s_f, r_f,
 ):
     groups = lax.axis_size("body")
@@ -145,51 +145,55 @@
 
     row8 = lax.broadcasted_iota(jnp.int32, (8, 128), 0)
 
-    def put_target(ref, at, x, y, zz, top, use_z=True):
+    def put_target(ref, half, at, x, y, zz, use_z=True):
         m = x * x + y * y + zz * zz + SOFTEN
-        o = 0 if top else 4
-        t = jnp.where(row8 == o, -2.0 * x, 0.0)
-        t = jnp.where(row8 == o + 1, -2.0 * y, t)
+        r = jnp.where(row8 < 4, row8, row8 - 4)
+        u = jnp.where(r == 0, -2.0 * x, jnp.where(r == 1, -2.0 * y, 0.0))
         if use_z:
-            t = jnp.where(row8 == o + 2, -2.0 * zz, t)
-        t = jnp.where(row8 == o + 3, 1.0, t)
-        t = jnp.where(row8 == 4 - o, m, t)
-        t1, t2, t3 = split3(t)
-        ref[:, 128 * at : 128 * at + 128] = jnp.concatenate(
-            [t1, t2, t1, t2, t3, t1], axis=0
-        ).astype(BF16)
+            u = jnp.where(r == 2, -2.0 * zz, u)
+        u = jnp.where(row8 == 3, 1.0, jnp.where(row8 == 7, m, u))
+        u1, u2, u3 = split3(u)
+        a = jnp.where((row8 < 4) | (row8 == 7), u1, u2)
+        b = jnp.where(row8 == 7, u2, a)
+        c = jnp.where((row8 < 3) | (row8 == 7), u3, u1)
+        t = [a, b, c]
+        zero = [jnp.zeros((8, 128), F32)] * 3
+        t = t + zero if half == 0 else zero + t
+        ref[:, 128 * at : 128 * at + 128] = jnp.concatenate(t, axis=0).astype(BF16)
 
     def spread(ref, r):
         return jnp.broadcast_to(ref[r : r + 1, :], (8, 128))
 
-    def target(b, at, ref, r, shift):
+    def target(ref, b, at, points, r, shift):
         put_target(
-            tgt.at[b], at, spread(ref, r) + 2.0 * shift, spread(ref, r + 1),
-            spread(ref, r + 2), b != 1,
+            ref, b % 2, at, spread(points, r) + 2.0 * shift, spread(points, r + 1),
+            spread(points, r + 2),
         )
 
     mine = pay.at[0, 0]
     for b in range(3):
-        for t in range(3):
-            target(b, 4 + t, mine, 24 + 4 * t, t - b)
+        for t in range(2):
+            target(tgt.at[b], b, 4 + t, mine, 24 + 4 * t, t - b)
+        target(tgp.at[b // 2], b, b % 2, mine, 32, 2 - b)
         put_target(
-            tgt.at[b], 7, spread(mine, 36) + 2.0 * (1 - b), spread(mine, 37),
-            jnp.full((8, 128), DEPTH, F32), b != 1,
+            tgv.at[b // 2], b % 2, b % 2, spread(mine, 36) + 2.0 * (1 - b),
+            spread(mine, 37), jnp.full((8, 128), DEPTH, F32),
         )
     for t in range(3):
         put_target(
-            tgf, t, spread(mine, 24 + 4 * t) + 2.0 * (t - 1), spread(mine, 25 + 4 * t),
-            spread(mine, 26 + 4 * t) - DEPTH, False, use_z=False,
-        )
-
-    acc[...] = jnp.zeros_like(acc)
-    accf[...] = jnp.zeros_like(accf)
+            tgf if t < 2 else tgp.at[1], 1, t if t < 2 else 1,
+            spread(mine, 24 + 4 * t) + 2.0 * (t - 1), spread(mine, 25 + 4 * t),
+            spread(mine, 26 + 4 * t) - DEPTH, use_z=False,
+        )
+
+    for ref in (acc, accp, accf, accv, accw):
+        ref[...] = jnp.zeros_like(ref)
 
     points(0).wait_recv()
     points(1).wait_recv()
     for b in range(3):
         for at, (side, t) in enumerate(CROSS[b]):
-            target(b, at, nbr.at[0 if side < 0 else 1], 4 * t, 3 * side + t - b)
+            target(tgt.at[b], b, at, nbr.at[0 if side < 0 else 1], 4 * t, 3 * side + t - b)
 
     row = lax.broadcasted_iota(jnp.int32, (8, 256), 0)
 
@@ -197,17 +201,21 @@
         return jnp.concatenate([pay[o, 0, r : r + 8, :], pay[o, 1, r : r + 8, :]], axis=1)
 
     def sources(o):
-        p, q = both(o, 24), both(o, 32)
-        low = row < 4
-        one4 = jnp.where(row == 4, 1.0, 0.0)
-        one0 = jnp.where(row == 0, 1.0, 0.0)
-        for i, c in enumerate(
-            (jnp.where(low, p, one4), jnp.where(low, one0, p),
-             jnp.where(low, q, one4), jnp.where(low, one0, q))
-        ):
-            c1, c2, c3 = split3(c)
-            f = jnp.concatenate([c1, c1, c2, c2, c1, c3], axis=0)
-            ft[o, i] = f.T.astype(BF16)
+        made = []
+        for i, p in enumerate((both(o, 24), both(o, 32))):
+            q = pltpu.roll(p, 4, 0)
+            groups = []
+            for lo, hi in ((p, q), (q, p)):
+                e = jnp.where(row < 4, lo, jnp.where(row < 7, hi, 1.0))
+                e1, e2, e3 = split3(e)
+                last = row == 7
+                groups += [
+                    e1, jnp.where(last, 1.0, e2),
+                    jnp.where((row < 3) | last, e1, e3),
+                ]
+            made.append(jnp.concatenate(groups, axis=0).T.astype(BF16))
+            ft[o, i] = made[i]
+        return made
 
     def sweep(features, targets, lhs, cubed=False):
         total = None
@@ -225,24 +233,31 @@
             total = part if total is None else total + part
         return total
 
-    def cross_step(k, carry):
-        o = order(k)
-
-        @pl.when(k < nz - 1)
+    def main_step(j, carry):
+        chips = [order(2 * j), order(2 * j + 1)]
+
+        @pl.when(j < nz // 2 - 1)
         def _():
-            ahead = order(k + 1)
-            direct(ahead).wait_recv()
-            relay(ahead).start()
-
-        relay(o).wait_recv()
-        sources(o)
+            for k in (2, 3):
+                ahead = order(2 * j + k)
+                direct(ahead).wait_recv()
+                relay(ahead).start()
+
+        for o in chips:
+            relay(o).wait_recv()
+        made = [sources(o) for o in chips]
+        lhs = [[split2(both(o, 8 * b)) for b in range(3)] for o in chips]
         for b in range(3):
-            lhs = split2(both(o, 8 * b))
-            for n in (0, 256):
-                acc[b, :, n : n + 256] += sweep(ft.at[o, b], tgt[b, :, n : n + 256], lhs)
+            for n in (0, 256, 512):
+                block = pl.ds(n, 256)
+                acc[b, :, block] += sum(
+                    sweep(made[i][b // 2], tgt[b, :, block], lhs[i][b]) for i in range(2)
+                )
         return carry
 
-    lax.fori_loop(0, nz, cross_step, 0)
+    direct(1).wait_recv()
+    relay(1).start()
+    lax.fori_loop(0, nz // 2, main_step, 0)
 
     def result(b, at):
         lanes = pl.ds(128 * at, 128)
@@ -259,17 +274,20 @@
     give_back(0).start()
     give_back(1).start()
 
-    def own_step(o, carry):
-        for b in range(3):
-            lhs = split2(both(o, 8 * b))
-            for n, width in ((512, 256), (768, 128)):
-                acc[b, :, n : n + width] += sweep(ft.at[o, b], tgt[b, :, n : n + width], lhs)
-        lhs = split2(both(o, 32))
-        for n, width in ((0, 256), (256, 128)):
-            accf[:, n : n + width] += sweep(ft.at[o, 3], tgf[:, n : n + width], lhs)
+    def own_step(j, carry):
+        first, second, third = 0.0, 0.0, 0.0
+        for o in (2 * j, 2 * j + 1):
+            surface = split2(both(o, 32))
+            w = [split2(both(o, 8 * b)) for b in range(3)]
+            first += sweep(ft[o, 0], tgp[0], jnp.concatenate([w[0], w[1]], axis=0))
+            second += sweep(ft[o, 1], tgp[1], jnp.concatenate([w[2], surface], axis=0))
+            third += sweep(ft[o, 1], tgf[...], surface)
+        accp[0] += first
+        accp[1] += second
+        accf[...] += third
         return carry
 
-    lax.fori_loop(0, nz, own_step, 0)
+    lax.fori_loop(0, nz // 2, own_step, 0)
 
     give_back(0).wait_recv()
     give_back(1).wait_recv()
@@ -278,33 +296,47 @@
     for t in range(3):
         total = reti[0, t] + reti[1, t]
         for b in range(3):
-            r = result(b, 4 + t)
+            if t < 2:
+                r = result(b, 4 + t)
+            else:
+                top, lanes = 16 * (b % 2), pl.ds(128 * (b % 2), 128)
+                r = accp[b // 2, top : top + 8, lanes] + accp[b // 2, top + 8 : top + 16, lanes]
             total += r if b == t else r * allowed(min(b, t), max(b, t))
-        surface = accf[6:7, 128 * t : 128 * t + 128] + accf[14:15, 128 * t : 128 * t + 128]
+        if t < 2:
+            surface = accf[6:7, 128 * t : 128 * t + 128] + accf[14:15, 128 * t : 128 * t + 128]
+        else:
+            surface = accp[1, 22:23, 128:256] + accp[1, 30:31, 128:256]
         total += jnp.where(row8 == 0, surface, 0.0)
         pot[t] = total
         for k in range(3):
             an = bn[k, t : t + 1, :] * bp[3, t : t + 1, :]
             column = jnp.sum(total * an, axis=1, keepdims=True)
-            packed = jnp.where(lane == 16 * row8 + 3 * t + k, column, packed)
+            packed = jnp.where(lane == 8 * (3 * t + k) + row8, column, packed)
     frc[s] = jnp.sum(packed, axis=0, keepdims=True)
     for d in range(1, tiles):
         forces(d, s).start()
 
-    def velocity_step(o, carry):
-        for b in range(3):
-            tile = both(o, 24 if b < 2 else 32)
-            w0 = jnp.broadcast_to(both(o, 8 * b)[0:1, :], (8, 256))
-            r = 4 if b == 1 else 0
-            lhs = split2(w0 * jnp.where(row == r + 3, 1.0, tile))
-            acc[b, :, 896:1024] += sweep(ft.at[o, b], tgt[b, :, 896:1024], lhs, cubed=True)
+    def velocity_step(j, carry):
+        first, second = 0.0, 0.0
+        for o in (2 * j, 2 * j + 1):
+            lhs = []
+            for b in range(3):
+                tile = both(o, 24 if b < 2 else 32)
+                w0 = jnp.broadcast_to(both(o, 8 * b)[0:1, :], (8, 256))
+                lhs.append(split2(w0 * jnp.where(row == (7 if b == 1 else 3), 1.0, tile)))
+            first += sweep(ft[o, 0], tgv[0], jnp.concatenate(lhs[:2], axis=0), cubed=True)
+            second += sweep(ft[o, 1], tgv[1, :, 0:128], lhs[2], cubed=True)
+        accv[...] += first
+        accw[...] += second
         return carry
 
-    lax.fori_loop(0, nz, velocity_step, 0)
+    lax.fori_loop(0, nz // 2, velocity_step, 0)
 
     v = [jnp.zeros((1, 128), F32)] * 3
     for b in range(3):
-        moments = result(b, 7)
+        ref = accv if b < 2 else accw
+        top, lanes = 16 * (b % 2), pl.ds(128 * (b % 2), 128)
+        moments = ref[top : top + 8, lanes] + ref[top + 8 : top + 16, lanes]
         r = 4 if b == 1 else 0
         point = (pay[0, 0, 36:37, :] + 2.0 * (1 - b), pay[0, 0, 37:38, :], DEPTH)
         for i in range(3):
@@ -319,12 +351,10 @@
     whole = frc[0]
     for i in range(1, tiles):
         whole = whole + frc[i]
-    whole = jnp.broadcast_to(whole, (8, 128))
     for t in range(3):
         for k in range(3):
-            force[t, :, k : k + 1] = jnp.sum(
-                jnp.where(lane == 16 * row8 + 3 * t + k, whole, 0.0), axis=1, keepdims=True
-            )
+            at = 8 * (3 * t + k)
+            force[t, k : k + 1, :] = whole[:, at : at + 8]
 
     for i in range(2):
         points(i).wait_send()
@@ -337,28 +367,40 @@
         forces(d, s).wait_send()
 
 
+def write_out(pot, force, fsn, pot_out, force_out, fsn_out):
+    pot_out[...] = pot[...]
+    force_out[...] = force[...]
+    fsn_out[...] = fsn[...]
+
+
 def on_device(bp, bn, fsp, fst, pairs):
     nz = lax.axis_size("surf") // 2
     tiles = 2 * nz
     dma = pltpu.SemaphoreType.DMA
     vmem = pl.BlockSpec(memory_space=pltpu.VMEM)
-    return pl.pallas_call(
+    shapes = (
+        jax.ShapeDtypeStruct((3, 8, 128), F32),
+        jax.ShapeDtypeStruct((3, 3, 8), F32),
+        jax.ShapeDtypeStruct((2, 128), F32),
+    )
+    outs = pl.pallas_call(
         functools.partial(kernel, nz),
-        out_shape=(
-            jax.ShapeDtypeStruct((3, 8, 128), F32),
-            jax.ShapeDtypeStruct((3, 8, 3), F32),
-            jax.ShapeDtypeStruct((2, 128), F32),
-        ),
+        out_shape=shapes,
         in_specs=[vmem] * 5,
         out_specs=(vmem,) * 3,
         scratch_shapes=[
             pltpu.VMEM((nz, 2, 40, 128), F32),
             pltpu.VMEM((2, 16, 128), F32),
-            pltpu.VMEM((3, 48, 1024), BF16),
-            pltpu.VMEM((48, 384), BF16),
-            pltpu.VMEM((nz, 4, 256, 48), BF16),
-            pltpu.VMEM((3, 16, 1024), F32),
-            pltpu.VMEM((16, 384), F32),
+            pltpu.VMEM((3, 48, 768), BF16),
+            pltpu.VMEM((2, 48, 256), BF16),
+            pltpu.VMEM((48, 256), BF16),
+            pltpu.VMEM((2, 48, 256), BF16),
+            pltpu.VMEM((nz, 2, 256, 48), BF16),
+            pltpu.VMEM((3, 16, 768), F32),
+            pltpu.VMEM((2, 32, 256), F32),
+            pltpu.VMEM((16, 256), F32),
+            pltpu.VMEM((32, 256), F32),
+            pltpu.VMEM((16, 128), F32),
             pltpu.VMEM((2, 3, 8, 128), F32),
             pltpu.VMEM((2, 3, 8, 128), F32),
             pltpu.VMEM((16, 128), F32),
@@ -370,6 +412,10 @@
         compiler_params=pltpu.CompilerParams(collective_id=0, has_side_effects=True),
         name="section",
     )(bp, bn, fsp, fst, pairs.T)
+    pot, force, fsn = pl.pallas_call(
+        write_out, out_shape=shapes, in_specs=[vmem] * 3, out_specs=(vmem,) * 3, name="write_out"
+    )(*outs)
+    return pot, force.transpose(0, 2, 1), fsn
 
 
 def solution(mesh):

time: 52.9 us -> 39.5 us (0.75)
  Pallas kernels: 49.4 us -> 38.6 us
  local copies, waits for them, and re-layouts: 2.59 us -> 0 us
    pallas_call x1 -> x2, Pallas kernels: 49.4 us -> 38.6 us  [the longest x1 37.3 us: on_device(): pl.pallas_call(functools.partial(kernel, nz), out_shape=shapes, in_specs=...]
    pallas_call x1 -> x0, local copies, waits for them, and re-layouts: 1.39 us -> none  [on_device(): pl.pallas_call(functools.partial(kernel, nz), out_shape=(jax.ShapeDtypeSt...]
    unnamed x6 -> x0, local copies, waits for them, and re-layouts: 1.2 us -> none
where the time goes in v1:
time: 39.5 us; the launch traced here: 39.2 us
  Pallas kernels  38.6 us (98%)
  between operations  0.64 us (2%)
    pallas_call x1, Pallas kernels, on_device(): pl.pallas_call(functools.partial(kernel, nz), out_shape=shapes, in_specs=...  37.3 us
    pallas_call x1, Pallas kernels, on_device(): pl.pallas_call(write_out, out_shape=shapes, in_specs=[vmem] * 3, out_spec...  1.33 us

profile of v1, /device:TPU:1, one launch (start us, length us, event | category | flops | bytes accessed | tf_op | source)
XLA Modules:
  0.0 39.2 jit_solution(3591857969247273366)
XLA Ops:
  0.6 37.3 %section.1 = (f32[3,8,128]{2,1,0:T(8,128)}, f32[3,3,8]{2,1,0:T(4,128)}, f32[2,128]{1,0:T(2,128)}) custom-call(f32[12,3,128]{2,1,0:T(4,128)} %bp.1, f32[3,3,128]{2,1,0:T(4,128)} %bn.1, f32[4,128]{1,0:T(4,128)} %fsp.1, f32[2,128]{1,0:T(2,128)} %fst.1, s32[2,72]{1,0:T(2,128)} %bitcast.2), custom_call_target="tpu_custom_call" | custom-call | tf_op jit(solution)/shard_map/section/pallas_call | solution.py:386
  37.9 1.3 %write_out.1 = (f32[3,8,128]{2,1,0:T(8,128)}, f32[3,3,8]{2,1,0:T(4,128)}, f32[2,128]{1,0:T(2,128)}) custom-call(f32[3,8,128]{2,1,0:T(8,128)} %get-tuple-element.9.pot, f32[3,3,8]{2,1,0:T(4,128)} %get-tuple-element.10.force, f32[2,128]{1,0:T(2,128)} %get-tuple-element.11.fsn), custom_call_target="tpu_custom_call" | custom-call | tf_op jit(solution)/shard_map/write_out/pallas_call | solution.py:415

commit v2 on v1

--- a/solution.py
+++ b/solution.py
@@ -41,10 +41,11 @@
 
 def kernel(
     nz,
+    bp_in, bn_in, fsp_in, fst_in, prs_in,
+    pot, force, fsn,
     bp, bn, fsp, fst, prs,
-    pot, force, fsn,
     pay, nbr, tgt, tgp, tgf, tgv, ft, acc, accp, accf, accv, accw, reto, reti, msk, frc,
-    s_dir, r_dir, s_rel, r_rel, s_nb, r_nb, s_ret, r_ret, s_f, r_f,
+    s_in, s_dir, r_dir, s_rel, r_rel, s_nb, r_nb, s_ret, r_ret, s_f, r_f,
 ):
     groups = lax.axis_size("body")
     tiles = 2 * nz
@@ -60,8 +61,37 @@
         pl.semaphore_signal(
             barrier, inc=1, device_id=(g, lax.rem(s + d, tiles)), device_id_type=MESH
         )
-    for other in (following, preceding):
-        pl.semaphore_signal(barrier, inc=1, device_id=(other, s), device_id_type=MESH)
+    has_following, has_preceding = g < groups - 1, g > 0
+
+    @pl.when(has_following)
+    def _():
+        pl.semaphore_signal(barrier, inc=1, device_id=(following, s), device_id_type=MESH)
+
+    @pl.when(has_preceding)
+    def _():
+        pl.semaphore_signal(barrier, inc=1, device_id=(preceding, s), device_id_type=MESH)
+
+    inputs = [
+        pltpu.make_async_copy(a, b, s_in.at[i])
+        for i, (a, b) in enumerate(
+            ((bp_in, bp), (fsp_in, fsp), (prs_in, prs), (bn_in, bn), (fst_in, fst))
+        )
+    ]
+    for copy in inputs:
+        copy.start()
+
+    @pl.when(g == 0)
+    def _():
+        nbr[0] = jnp.zeros_like(nbr[0])
+        reti[0] = jnp.zeros_like(reti[0])
+
+    @pl.when(g == groups - 1)
+    def _():
+        nbr[1] = jnp.zeros_like(nbr[1])
+        reti[1] = jnp.zeros_like(reti[1])
+
+    inputs[0].wait()
+    inputs[1].wait()
 
     base = 6.0 * g.astype(F32)
     area = bp[3]
@@ -80,7 +110,10 @@
     for i, v in enumerate((fx, fy, fsp[2:3, :] * fsp[3:4, :], fx * fx + fy * fy)):
         pay[0, 0, 36 + i : 37 + i, :] = v
 
-    pl.semaphore_wait(barrier, tiles + 1)
+    pl.semaphore_wait(
+        barrier,
+        tiles - 1 + (g + groups - 1) // groups + (2 * groups - 2 - g) // groups,
+    )
 
     def direct(o):
         return pltpu.make_async_remote_copy(
@@ -96,6 +129,15 @@
             device_id=(g, partner), device_id_type=MESH,
         )
 
+    far = nz // 2
+
+    def across():
+        return pltpu.make_async_remote_copy(
+            src_ref=pay.at[0, 0], dst_ref=pay.at[far, 1],
+            send_sem=s_rel.at[far], recv_sem=r_rel.at[far],
+            device_id=(g, 2 * lax.rem(z + far, nz) + 1 - core), device_id_type=MESH,
+        )
+
     def points(i):
         return pltpu.make_async_remote_copy(
             src_ref=pay.at[0, 0, pl.ds(24, 16)], dst_ref=nbr.at[i],
@@ -121,13 +163,18 @@
         half = (k + 1) // 2
         return jnp.where(lax.rem(k, 2) == 1, half, lax.rem(nz - half, nz))
 
-    points(0).start()
-    points(1).start()
+    def sides(first, second):
+        pl.when(has_following)(first)
+        pl.when(has_preceding)(second)
+
+    sides(lambda: points(0).start(), lambda: points(1).start())
     relay(0).start()
     for h in range(1, nz // 2 + 1):
         direct(h).start()
         if h != nz - h:
             direct(nz - h).start()
+    across().start()
+    inputs[2].wait()
 
     row_i = lax.broadcasted_iota(jnp.int32, (16, prs.shape[1]), 0)
     first = jnp.full(row_i.shape, -9, jnp.int32)
@@ -189,8 +236,7 @@
     for ref in (acc, accp, accf, accv, accw):
         ref[...] = jnp.zeros_like(ref)
 
-    points(0).wait_recv()
-    points(1).wait_recv()
+    sides(lambda: points(1).wait_recv(), lambda: points(0).wait_recv())
     for b in range(3):
         for at, (side, t) in enumerate(CROSS[b]):
             target(tgt.at[b], b, at, nbr.at[0 if side < 0 else 1], 4 * t, 3 * side + t - b)
@@ -233,31 +279,35 @@
             total = part if total is None else total + part
         return total
 
-    def main_step(j, carry):
-        chips = [order(2 * j), order(2 * j + 1)]
-
-        @pl.when(j < nz // 2 - 1)
+    def arrive(k):
+        direct(order(k)).wait_recv()
+
+        @pl.when(k < nz - 1)
         def _():
-            for k in (2, 3):
-                ahead = order(2 * j + k)
-                direct(ahead).wait_recv()
-                relay(ahead).start()
-
+            relay(order(k)).start()
+
+    def meet(chips, blocks):
         for o in chips:
             relay(o).wait_recv()
         made = [sources(o) for o in chips]
         lhs = [[split2(both(o, 8 * b)) for b in range(3)] for o in chips]
         for b in range(3):
-            for n in (0, 256, 512):
+            for n in blocks:
                 block = pl.ds(n, 256)
                 acc[b, :, block] += sum(
                     sweep(made[i][b // 2], tgt[b, :, block], lhs[i][b]) for i in range(2)
                 )
+
+    def main_step(j, carry):
+        arrive(2 * j + 2)
+        arrive(2 * j + 3)
+        meet([order(2 * j), order(2 * j + 1)], (0, 256, 512))
         return carry
 
-    direct(1).wait_recv()
-    relay(1).start()
-    lax.fori_loop(0, nz // 2, main_step, 0)
+    arrive(1)
+    lax.fori_loop(0, nz // 2 - 1, main_step, 0)
+    last = [order(nz - 2), order(nz - 1)]
+    meet(last, (0, 256))
 
     def result(b, at):
         lanes = pl.ds(128 * at, 128)
@@ -271,8 +321,7 @@
                     pair = (b, 3 + t) if side > 0 else (t - 3, b)
                     total += result(b, CROSS[b].index((side, t))) * allowed(*pair)
             reto[i, t] = total
-    give_back(0).start()
-    give_back(1).start()
+    sides(lambda: give_back(0).start(), lambda: give_back(1).start())
 
     def own_step(j, carry):
         first, second, third = 0.0, 0.0, 0.0
@@ -288,9 +337,13 @@
         return carry
 
     lax.fori_loop(0, nz // 2, own_step, 0)
-
-    give_back(0).wait_recv()
-    give_back(1).wait_recv()
+    for b in range(3):
+        acc[b, :, 512:768] += sum(
+            sweep(ft[o, b // 2], tgt[b, :, 512:768], split2(both(o, 8 * b))) for o in last
+        )
+
+    sides(lambda: give_back(1).wait_recv(), lambda: give_back(0).wait_recv())
+    inputs[3].wait()
     lane = lax.broadcasted_iota(jnp.int32, (8, 128), 1)
     packed = jnp.zeros((8, 128), F32)
     for t in range(3):
@@ -341,6 +394,7 @@
         point = (pay[0, 0, 36:37, :] + 2.0 * (1 - b), pay[0, 0, 37:38, :], DEPTH)
         for i in range(3):
             v[i] = v[i] + (moments[r + i : r + i + 1] - point[i] * moments[r + 3 : r + 4])
+    inputs[4].wait()
     speed_sq = v[0] * v[0] + v[1] * v[1] + v[2] * v[2]
     phi, eta = fst[0:1, :], fst[1:2, :]
     fsn[0:1, :] = phi + STEP * (-GRAVITY * eta - 0.5 * speed_sq)
@@ -356,11 +410,10 @@
             at = 8 * (3 * t + k)
             force[t, k : k + 1, :] = whole[:, at : at + 8]
 
-    for i in range(2):
-        points(i).wait_send()
-        give_back(i).wait_send()
+    sides(lambda: points(0).wait_send(), lambda: points(1).wait_send())
+    sides(lambda: give_back(0).wait_send(), lambda: give_back(1).wait_send())
     for o in range(nz):
-        relay(o).wait_send()
+        (across() if o == far else relay(o)).wait_send()
         if o:
             direct(o).wait_send()
     for d in range(1, tiles):
@@ -386,9 +439,14 @@
     outs = pl.pallas_call(
         functools.partial(kernel, nz),
         out_shape=shapes,
-        in_specs=[vmem] * 5,
+        in_specs=[pl.BlockSpec(memory_space=pl.ANY)] * 5,
         out_specs=(vmem,) * 3,
         scratch_shapes=[
+            pltpu.VMEM(bp.shape, F32),
+            pltpu.VMEM(bn.shape, F32),
+            pltpu.VMEM(fsp.shape, F32),
+            pltpu.VMEM(fst.shape, F32),
+            pltpu.VMEM(pairs.shape[::-1], jnp.int32),
             pltpu.VMEM((nz, 2, 40, 128), F32),
             pltpu.VMEM((2, 16, 128), F32),
             pltpu.VMEM((3, 48, 768), BF16),
@@ -405,7 +463,7 @@
             pltpu.VMEM((2, 3, 8, 128), F32),
             pltpu.VMEM((16, 128), F32),
             pltpu.VMEM((tiles, 1, 128), F32),
-            dma((nz,)), dma((nz,)), dma((nz,)), dma((nz,)),
+            dma((5,)), dma((nz,)), dma((nz,)), dma((nz,)), dma((nz,)),
             dma((2,)), dma((2,)), dma((2,)), dma((2,)),
             dma((tiles,)), dma((tiles,)),
         ],

time: 39.5 us -> 35.9 us (0.909)
  the two profiles are of different devices: /device:TPU:1 before, /device:TPU:56 now
where the time goes in v2:
time: 35.9 us; the launch traced here: 35.7 us
  Pallas kernels  35.1 us (98%)
  between operations  0.64 us (2%)
    pallas_call x1, Pallas kernels, on_device(): pl.pallas_call(functools.partial(kernel, nz), out_shape=shapes, in_specs=...  33.7 us
    pallas_call x1, Pallas kernels, on_device(): pl.pallas_call(write_out, out_shape=shapes, in_specs=[vmem] * 3, out_spec...  1.33 us

profile of v2, /device:TPU:56, one launch (start us, length us, event | category | flops | bytes accessed | tf_op | source)
XLA Modules:
  0.0 35.7 jit_solution(4171866864731217408)
XLA Ops:
  0.6 33.7 %section.1 = (f32[3,8,128]{2,1,0:T(8,128)}, f32[3,3,8]{2,1,0:T(4,128)}, f32[2,128]{1,0:T(2,128)}) custom-call(f32[12,3,128]{2,1,0:T(4,128)} %bp_in.1, f32[3,3,128]{2,1,0:T(4,128)} %bn_in.1, f32[4,128]{1,0:T(4,128)} %fsp_in.1, f32[2,128]{1,0:T(2,128)} %fst_in.1, s32[2,72]{1,0:T(2,128)} %bitcast.2), custom_call_target="tpu_custom_call" | custom-call | tf_op jit(solution)/shard_map/section/pallas_call | solution.py:439
  34.4 1.3 %write_out.1 = (f32[3,8,128]{2,1,0:T(8,128)}, f32[3,3,8]{2,1,0:T(4,128)}, f32[2,128]{1,0:T(2,128)}) custom-call(f32[3,8,128]{2,1,0:T(8,128)} %get-tuple-element.9.pot, f32[3,3,8]{2,1,0:T(4,128)} %get-tuple-element.10.force, f32[2,128]{1,0:T(2,128)} %get-tuple-element.11.fsn), custom_call_target="tpu_custom_call" | custom-call | tf_op jit(solution)/shard_map/write_out/pallas_call | solution.py:473
